TPU v7x, 32 devices: a whole 2x2x4 slice. The times are simulated.
32 devices in a mesh: coarse: 8 (over z, y), fine: 4 (over x, core).
Axes of the slice: x: 2, y: 2, z: 4, core: 2. Of those that a mesh axis runs over, the one named last changes fastest.
Arguments:
- right_side: float32 [64, 32, 128], P('coarse', 'fine'), may hold values from -6 to 6
- coefficient_index: int32 [64, 32, 128], P('coarse', 'fine'), may hold values from 0 to 15
- material_coefficients: float32 [16], replicated, may hold values from 0.02 to 0.5
- block_cells: int32 [8, 4, 64, 128], P('coarse', 'fine'), may hold values from 0 to 8191, as said below
- block_inverses: float32 [8, 4, 64, 128, 128], P('coarse', 'fine'), as said below
- aggregate_map: int32 [64, 32, 128], P('coarse', 'fine'), may hold values from 0 to 15, as said below
- coarse_diagonal: float32 [8, 4, 16], P('coarse', 'fine'), may hold values from 0.1 to 8
Outputs:
- solution: float32 [64, 32, 128], P('coarse', 'fine')
- residual: float32 [64, 32, 128], P('coarse', 'fine')
- direction: float32 [64, 32, 128], P('coarse', 'fine')
Inputs may be any that keep to these rules, and one draw needn't show every extreme that they name: `block_cells`: each device block's 64 x 128 entries list each of its local cell numbers exactly once. `block_inverses`: every 128 x 128 matrix is symmetric positive definite. A cell with third index j has aggregate_map equal to j // 8 - 1, j // 8 or j // 8 + 1.
All inputs are finite; a program needn't handle non-finite values.
Results may differ from a plain program's by a relative error of at most 0.00016.
Values sent between devices are 32-bit elements; how exact they have to be, the bound alone decides.
A program may use at most 64 MiB of HBM per device.

v0:
```python
import jax
import jax.numpy as jnp
from jax import lax
from jax.sharding import PartitionSpec as P

AGG = 8
ITERS = 2
SWEEPS = 4


omega = 0.8
restrict_scale = 0.25


def with_halo(cells, sides, width):
    for axis, dim in sides:
        count = lax.axis_size(axis)
        ends = count - 1
        head = lax.slice_in_dim(cells, 0, width, axis=dim)
        tail = lax.slice_in_dim(cells, cells.shape[dim] - width, cells.shape[dim], axis=dim)
        cells = jnp.concatenate(
            [
                lax.ppermute(tail, axis, [(i, (i + 1) % count) for i in range(ends)]),
                cells,
                lax.ppermute(head, axis, [((i + 1) % count, i) for i in range(ends)]),
            ],
            axis=dim,
        )
    return cells


def neighbours():
    result = []
    for shift_x in (-1, 0, 1):
        for shift_z in (-1, 0, 1):
            for shift_y in (-1, 0, 1):
                reach = abs(shift_x) + abs(shift_z) + abs(shift_y)
                if reach > 0:
                    result.append((shift_x, shift_z, shift_y, 0.5 ** (reach - 1)))
    return result


def window(padded, shift_x, shift_z, shift_y, shape):
    return padded[
        1 + shift_x : 1 + shift_x + shape[0],
        1 + shift_z : 1 + shift_z + shape[1],
        1 + shift_y : 1 + shift_y + shape[2],
    ]


def pad_last(array):
    return jnp.pad(array, ((0, 0), (0, 0), (1, 1)))


def seven_point(padded, diagonal, guess):
    beside = padded[2:, 1:-1, 1:-1] + padded[:-2, 1:-1, 1:-1]
    beside = beside + padded[1:-1, 2:, 1:-1] + padded[1:-1, :-2, 1:-1]
    beside = beside + padded[1:-1, 1:-1, 2:] + padded[1:-1, 1:-1, :-2]
    return (6.0 + diagonal) * guess - beside


def jacobi(source, diagonal, operate_coarse):
    scaled = 6.0 + diagonal
    guess = omega * source / scaled
    for sweep in range(SWEEPS - 1):
        guess = guess + omega * (source - operate_coarse(guess)) / scaled
    return guess


def displace(values, move):
    if move > 0:
        return jnp.pad(values[:-move], (move, 0))
    if move < 0:
        return jnp.pad(values[-move:], (0, -move))
    return values


def shards(
    right_side,
    coefficient_index,
    material_coefficients,
    block_cells,
    block_inverses,
    aggregate_map,
    coarse_diagonal,
):
    extent_x, extent_z, extent_y = right_side.shape
    shape = right_side.shape
    cells = extent_x * extent_z * extent_y
    boxes = extent_y // AGG
    table = jnp.arange(material_coefficients.shape[0], dtype=jnp.int32)
    kappa = jnp.sum(
        jnp.where(coefficient_index[..., None] == table, material_coefficients, 0.0), axis=-1
    )
    kappa_wide = pad_last(with_halo(kappa, (("coarse", 0), ("fine", 1)), 1))
    couplings = []
    centre = jnp.zeros(shape, jnp.float32)
    for shift_x, shift_z, shift_y, weight in neighbours():
        coupling = weight * 0.5 * (kappa + window(kappa_wide, shift_x, shift_z, shift_y, shape))
        couplings.append(coupling)
        centre = centre + coupling
    order = block_cells.reshape(cells)
    places = jnp.zeros((cells,), jnp.int32).at[order].set(jnp.arange(cells, dtype=jnp.int32))
    matrices = block_inverses.reshape(
        block_inverses.shape[2], block_inverses.shape[3], block_inverses.shape[4]
    )

    def block_apply(residual):
        picked = residual.reshape(cells)[order].reshape(matrices.shape[0], matrices.shape[1])
        product = jnp.einsum("bij,bj->bi", matrices, picked, precision=lax.Precision.HIGHEST)
        return product.reshape(cells)[places].reshape(shape)

    offset = aggregate_map - (jnp.arange(extent_y, dtype=jnp.int32) // AGG)[None, None, :]

    def restrict(residual):
        total = jnp.zeros((boxes,), jnp.float32)
        for move in (-1, 0, 1):
            masked = jnp.where(offset == move, residual, 0.0).reshape(
                extent_x, extent_z, boxes, AGG
            )
            total = total + displace(jnp.sum(masked, axis=(0, 1, 3)), move)
        return (restrict_scale * total).reshape(1, 1, boxes)

    def prolong(coarse):
        values = coarse.reshape(boxes)
        result = jnp.zeros(shape, jnp.float32)
        for move in (-1, 0, 1):
            repeated = jnp.repeat(displace(values, -move), AGG)
            result = jnp.where(offset == move, repeated[None, None, :], result)
        return result

    column_diagonal = lax.all_gather(coarse_diagonal, "fine", axis=1, tiled=True)

    def coarse_solve(source):
        group = lax.all_gather(source, "fine", axis=1, tiled=True)

        def operate_column(guess):
            edges = with_halo(guess, (("coarse", 0),), 1)
            wide = jnp.pad(edges, ((0, 0), (1, 1), (1, 1)))
            return seven_point(wide, column_diagonal, guess)

        whole = jacobi(group, column_diagonal, operate_column)
        return lax.dynamic_slice_in_dim(whole, lax.axis_index("fine"), 1, 1)

    def precondition(residual):
        return block_apply(residual) + prolong(coarse_solve(restrict(residual)))

    def norm_of(residual, smoothed):
        return lax.psum(jnp.sum(residual * smoothed), ("coarse", "fine"))

    solution = jnp.zeros(shape, jnp.float32)
    residual = right_side
    search = precondition(residual)
    current = norm_of(residual, search)
    for step in range(ITERS):
        operate_wide = pad_last(with_halo(search, (("coarse", 0), ("fine", 1)), 1))
        operate_total = centre * search
        for (
            operate_shift_x,
            operate_shift_z,
            operate_shift_y,
            operate_weight,
        ), operate_coupling in zip(neighbours(), couplings):
            operate_total = operate_total - operate_coupling * window(
                operate_wide, operate_shift_x, operate_shift_z, operate_shift_y, shape
            )
        alpha = current / lax.psum(jnp.sum(search * operate_total), ("coarse", "fine"))
        solution = solution + alpha * search
        residual = residual - alpha * operate_total
        smoothed = precondition(residual)
        following = norm_of(residual, smoothed)
        search = smoothed + following / current * search
        current = following
    return (solution, residual, search)


def solution(mesh):
    return jax.shard_map(
        shards,
        mesh=mesh,
        in_specs=(
            P("coarse", "fine", None),
            P("coarse", "fine", None),
            P(),
            P("coarse", "fine", None, None),
            P("coarse", "fine", None, None, None),
            P("coarse", "fine", None),
            P("coarse", "fine", None),
        ),
        out_specs=(P("coarse", "fine", None), P("coarse", "fine", None), P("coarse", "fine", None)),
        check_vma=False,
    )
```

profile of v0, /device:TPU:0, one launch (start us, length us, event | category | flops | bytes accessed | tf_op | source)
XLA Modules:
  0.0 643.6 jit_solution(8524950483401387286)
XLA Ops:
  0.7 0.8 select_reduce_fusion.9
  2.2 1.2 dynamic-slice
  4.3 8.3 %all-reduce.24 = f32[64]{0:T(128)S(1)} all-reduce(f32[64]{0:T(128)S(1)} %multiply_dynamic-update-slice_fusion.2), channel_id=2, replica_groups=mesh['coarse'=8,'fine'=4] {'fine'}, use_global_device_ids=true, to_apply=%add.24 | all-reduce | flops 64 | bytes 512
  12.7 5.2 all_gather.13
  17.9 1.3 collective-permute-start
  19.2 4.5 collective-permute-start.1
  23.7 1.0 select_reduce_fusion
  24.8 4.3 collective-permute-start.6
  29.1 1.3 collective-permute-start.7
  30.4 0.8 compare_select_fusion
  31.2 30.5 %scatter_custom_fusion = s32[8192]{0:T(1024)S(1)} fusion(s32[8192]{0:T(1024)S(1)} %bitcast.99, s32[8192]{0:T(1024)S(1)} %iota.12, s32[]{:T(128)} %constant.14.clone.1), kind=kCustom, calls=%fused_computation.232 | custom fusion | bytes 32772 | tf_op jit(solution)/shard_map/scatter | solution.py:103
  61.7 45.5 %gather_fusion = f32[8192]{0:T(1024)S(1)} fusion(f32[8192]{0:T(1024)S(1)} %bitcast.80, s32[8192]{0:T(1024)S(1)} %broadcast_clamp_fusion), kind=kCustom, calls=%fused_computation | custom fusion | bytes 98304 | tf_op jit(solution)/shard_map/gather | solution.py:109
  107.3 8.3 %fusion.4 = f32[64,1,128]{2,1,0:T(1,128)S(1)} fusion(f32[64,128,1]{1,2,0:T(1,128)S(1)} %bitcast.102, f32[1,1,64,128,128]{4,3,2,1,0:T(8,128)} %param.11), kind=kOutput, calls=%fused_computation.11 | convolution fusion | flops 12582912 | bytes 4259840 | tf_op jit(solution)/shard_map/bij,bj->bi/dot_general | solution.py:110
  115.8 1.3 collective-permute-start.2
  117.1 5.2 collective-permute-start.3
  122.3 1.3 collective-permute-done.3
  123.7 1.3 collective-permute-start.4
  125.0 5.4 collective-permute-start.5
  130.5 45.5 %gather_fusion.1 = f32[8192]{0:T(1024)S(1)} fusion(f32[8192]{0:T(1024)S(1)} %bitcast.83, s32[8192]{0:T(1024)S(1)} %fusion.7), kind=kCustom, calls=%fused_computation.1 | custom fusion | bytes 98304 | tf_op jit(solution)/shard_map/gather | solution.py:111
  176.9 5.1 collective-permute-start.10
  182.0 1.3 collective-permute-start.11
  183.3 1.3 collective-permute-start.8
  184.6 1.3 collective-permute-start.9
  185.9 1.6 collective-permute-done.11
  187.5 2.2 collective-permute-start.12
  189.7 1.3 collective-permute-start.13
  191.3 2.8 collective-permute-done.13
  194.2 1.0 multiply_reduce_fusion.3
  195.2 42.7 %all-reduce.27 = (f32[]{:T(128)}, f32[]{:T(128)}) all-reduce(f32[]{:T(128)} %get-tuple-element.10, f32[]{:T(128)} %get-tuple-element.9), channel_id=1, replica_groups=mesh['coarse'=8,'fine'=4] {'coarse','fine'}, use_global_device_ids=true, to_apply=%region_8.9 | all-reduce | flops 2 | bytes 16 | tf_op jit(solution)/shard_map/psum | solution.py:149
  240.2 7.2 %all-reduce.25 = f32[64]{0:T(128)S(1)} all-reduce(f32[64]{0:T(128)S(1)} %multiply_dynamic-update-slice_fusion.1), channel_id=3, replica_groups=mesh['coarse'=8,'fine'=4] {'fine'}, use_global_device_ids=true, to_apply=%add.25 | all-reduce | flops 64 | bytes 512
  247.5 1.3 collective-permute-start.14
  248.8 4.5 collective-permute-start.15
  253.3 1.3 collective-permute-done.15
  254.8 1.3 collective-permute-start.16
  256.1 4.8 collective-permute-start.17
  260.9 45.5 %gather_fusion.2 = f32[8192]{0:T(1024)S(1)} fusion(f32[8192]{0:T(1024)S(1)} %bitcast.81, s32[8192]{0:T(1024)S(1)} %broadcast_clamp_fusion), kind=kCustom, calls=%fused_computation.2 | custom fusion | bytes 98304 | tf_op jit(solution)/shard_map/gather | solution.py:109
  306.6 1.3 collective-permute-start.18
  307.9 5.6 collective-permute-start.19
  313.5 8.3 %fusion.2 = f32[64,1,128]{2,1,0:T(1,128)S(1)} fusion(f32[64,128,1]{1,2,0:T(1,128)S(1)} %bitcast.101, f32[1,1,64,128,128]{4,3,2,1,0:T(8,128)} %param.11), kind=kOutput, calls=%fused_computation.9 | convolution fusion | flops 12582912 | bytes 4259840 | tf_op jit(solution)/shard_map/bij,bj->bi/dot_general | solution.py:110
  321.8 45.5 %gather_fusion.3 = f32[8192]{0:T(1024)S(1)} fusion(f32[8192]{0:T(1024)S(1)} %bitcast.85, s32[8192]{0:T(1024)S(1)} %fusion.7), kind=kCustom, calls=%fused_computation.3 | custom fusion | bytes 98304 | tf_op jit(solution)/shard_map/gather | solution.py:111
  368.3 0.6 multiply_reduce_fusion.2
  368.9 42.1 %psum.37 = f32[]{:T(128)} all-reduce(f32[]{:T(128)} %multiply_reduce_fusion.2), channel_id=1, replica_groups=mesh['coarse'=8,'fine'=4] {'coarse','fine'}, use_global_device_ids=true, to_apply=%region_19.20 | all-reduce | flops 1 | bytes 8 | tf_op jit(solution)/shard_map/psum | solution.py:149
  412.4 4.5 collective-permute-start.20
  416.8 1.3 collective-permute-start.21
  418.2 4.2 collective-permute-done.21
  422.4 1.3 collective-permute-start.22
  423.7 1.3 collective-permute-start.23
  425.0 2.3 collective-permute-done.23
  427.4 1.0 multiply_reduce_fusion.1
  428.4 42.0 %psum.38 = f32[]{:T(128)} all-reduce(f32[]{:T(128)} %get-tuple-element.17), channel_id=1, replica_groups=mesh['coarse'=8,'fine'=4] {'coarse','fine'}, use_global_device_ids=true, to_apply=%region_21.22 | all-reduce | flops 1 | bytes 8 | tf_op jit(solution)/shard_map/psum | solution.py:167
  472.7 5.8 all-reduce.26
  478.6 1.3 collective-permute-start.24
  479.9 4.9 collective-permute-start.25
  484.8 1.3 collective-permute-done.25
  486.3 1.3 collective-permute-start.26
  487.6 5.4 collective-permute-start.27
  493.0 45.5 %gather_fusion.4 = f32[8192]{0:T(1024)S(1)} fusion(f32[8192]{0:T(1024)S(1)} %bitcast.82, s32[8192]{0:T(1024)S(1)} %broadcast_clamp_fusion), kind=kCustom, calls=%fused_computation.4 | custom fusion | bytes 98304 | tf_op jit(solution)/shard_map/gather | solution.py:109
  538.8 1.3 collective-permute-start.28
  540.1 5.7 collective-permute-start.29
  545.8 8.3 %fusion = f32[64,1,128]{2,1,0:T(1,128)S(1)} fusion(f32[64,128,1]{1,2,0:T(1,128)S(1)} %bitcast.100, f32[1,1,64,128,128]{4,3,2,1,0:T(8,128)} %param.11), kind=kOutput, calls=%fused_computation.7 | convolution fusion | flops 12582912 | bytes 4259840 | tf_op jit(solution)/shard_map/bij,bj->bi/dot_general | solution.py:110
  554.1 45.5 %gather_fusion.5 = f32[8192]{0:T(1024)S(1)} fusion(f32[8192]{0:T(1024)S(1)} %bitcast.84, s32[8192]{0:T(1024)S(1)} %fusion.7), kind=kCustom, calls=%fused_computation.5 | custom fusion | bytes 98304 | tf_op jit(solution)/shard_map/gather | solution.py:111
  600.5 0.6 multiply_reduce_fusion
  601.1 40.4 %psum.39 = f32[]{:T(128)} all-reduce(f32[]{:T(128)} %multiply_reduce_fusion), channel_id=1, replica_groups=mesh['coarse'=8,'fine'=4] {'coarse','fine'}, use_global_device_ids=true, to_apply=%region_29.30 | all-reduce | flops 1 | bytes 8 | tf_op jit(solution)/shard_map/psum | solution.py:149
  642.9 0.7 multiply_add_fusion
  (131 shorter events, 7.1 us)
Async XLA Ops:
  0.6 61.1 %copy-start = (f32[8,8,128]{2,1,0:T(8,128)S(1)}, f32[8,8,128]{2,1,0:T(8,128)}, u32[]{:S(2)}) copy-start(f32[8,8,128]{2,1,0:T(8,128)} %param.7) | copy-start | bytes 98308
  17.9 97.7 %collective-permute-start = (f32[1,4,16]{2,1,0:T(4,128)S(1)}, f32[1,4,16]{2,1,0:T(4,128)S(1)}, u32[]{:S(2)}, u32[]{:S(2)}) collective-permute-start(f32[1,4,16]{2,1,0:T(4,128)S(1)} %multiply_divide_fusion.2), channel_id=1, source_target_pairs={{4,0},{8,4},{12,8},{16,12},{20,16},{24,20},{28,24},{5,1},{9,5},{13... | collective-permute-start | bytes 776 | tf_op jit(solution)/shard_map/ppermute | solution.py:25
  19.2 96.4 %collective-permute-start.1 = (f32[1,4,16]{2,1,0:T(4,128)S(1)}, f32[1,4,16]{2,1,0:T(4,128)S(1)}, u32[]{:S(2)}, u32[]{:S(2)}) collective-permute-start(f32[1,4,16]{2,1,0:T(4,128)S(1)} %multiply_divide_fusion.2), channel_id=1, source_target_pairs={{0,4},{4,8},{8,12},{12,16},{16,20},{20,24},{24,28},{1,5},{5,9},{9,... | collective-permute-start | bytes 776 | tf_op jit(solution)/shard_map/ppermute | solution.py:23
  24.8 158.5 %collective-permute-start.6 = (f32[1,8,128]{2,1,0:T(8,128)S(1)}, f32[1,8,128]{2,1,0:T(8,128)S(1)}, u32[]{:S(2)}, u32[]{:S(2)}) collective-permute-start(f32[1,8,128]{2,1,0:T(8,128)S(1)} %get-tuple-element.40), channel_id=1, source_target_pairs={{0,4},{4,8},{8,12},{12,16},{16,20},{20,24},{24,28},{1,5},{5,9},{9,... | collective-permute-start | bytes 12296 | tf_op jit(solution)/shard_map/ppermute | solution.py:23
  29.1 154.2 %collective-permute-start.7 = (f32[1,8,128]{2,1,0:T(8,128)S(1)}, f32[1,8,128]{2,1,0:T(8,128)S(1)}, u32[]{:S(2)}, u32[]{:S(2)}) collective-permute-start(f32[1,8,128]{2,1,0:T(8,128)S(1)} %get-tuple-element.41), channel_id=1, source_target_pairs={{4,0},{8,4},{12,8},{16,12},{20,16},{24,20},{28,24},{5,1},{9,5},{13... | collective-permute-start | bytes 12296 | tf_op jit(solution)/shard_map/ppermute | solution.py:25
  115.8 6.5 %collective-permute-start.2 = (f32[1,4,16]{2,1,0:T(4,128)S(1)}, f32[1,4,16]{2,1,0:T(4,128)S(1)}, u32[]{:S(2)}, u32[]{:S(2)}) collective-permute-start(f32[1,4,16]{2,1,0:T(4,128)S(1)} %fusion.141), channel_id=1, source_target_pairs={{4,0},{8,4},{12,8},{16,12},{20,16},{24,20},{28,24},{5,1},{9,5},{13... | collective-permute-start | bytes 776 | tf_op jit(solution)/shard_map/ppermute | solution.py:25
  117.1 6.5 %collective-permute-start.3 = (f32[1,4,16]{2,1,0:T(4,128)S(1)}, f32[1,4,16]{2,1,0:T(4,128)S(1)}, u32[]{:S(2)}, u32[]{:S(2)}) collective-permute-start(f32[1,4,16]{2,1,0:T(4,128)S(1)} %fusion.141), channel_id=1, source_target_pairs={{0,4},{4,8},{8,12},{12,16},{16,20},{20,24},{24,28},{1,5},{5,9},{9,... | collective-permute-start | bytes 776 | tf_op jit(solution)/shard_map/ppermute | solution.py:23
  123.7 52.3 %collective-permute-start.4 = (f32[1,4,16]{2,1,0:T(4,128)S(1)}, f32[1,4,16]{2,1,0:T(4,128)S(1)}, u32[]{:S(2)}, u32[]{:S(2)}) collective-permute-start(f32[1,4,16]{2,1,0:T(4,128)S(1)} %fusion.140), channel_id=1, source_target_pairs={{4,0},{8,4},{12,8},{16,12},{20,16},{24,20},{28,24},{5,1},{9,5},{13... | collective-permute-start | bytes 776 | tf_op jit(solution)/shard_map/ppermute | solution.py:25
  125.0 51.0 %collective-permute-start.5 = (f32[1,4,16]{2,1,0:T(4,128)S(1)}, f32[1,4,16]{2,1,0:T(4,128)S(1)}, u32[]{:S(2)}, u32[]{:S(2)}) collective-permute-start(f32[1,4,16]{2,1,0:T(4,128)S(1)} %fusion.140), channel_id=1, source_target_pairs={{0,4},{4,8},{8,12},{12,16},{16,20},{20,24},{24,28},{1,5},{5,9},{9,... | collective-permute-start | bytes 776 | tf_op jit(solution)/shard_map/ppermute | solution.py:23
  176.9 9.0 %collective-permute-start.10 = (f32[1,8,128]{2,1,0:T(8,128)S(1)}, f32[1,8,128]{2,1,0:T(8,128)S(1)}, u32[]{:S(2)}, u32[]{:S(2)}) collective-permute-start(f32[1,8,128]{2,1,0:T(8,128)S(1)} %get-tuple-element.42), channel_id=1, source_target_pairs={{0,4},{4,8},{8,12},{12,16},{16,20},{20,24},{24,28},{1,5},{5,9},{9,... | collective-permute-start | bytes 12296 | tf_op jit(solution)/shard_map/ppermute | solution.py:23
  182.0 5.5 collective-permute-start.11
  183.3 7.7 %collective-permute-start.8 = (f32[10,1,128]{2,1,0:T(1,128)S(1)}, f32[10,1,128]{2,1,0:T(1,128)S(1)}, u32[]{:S(2)}, u32[]{:S(2)}) collective-permute-start(f32[10,1,128]{2,1,0:T(1,128)S(1)} %get-tuple-element.30), channel_id=1, source_target_pairs={{0,1},{1,2},{2,3},{4,5},{5,6},{6,7},{8,9},{9,10},{10,11},{12,13},{... | collective-permute-start | bytes 15368 | tf_op jit(solution)/shard_map/ppermute | solution.py:23
  184.6 6.4 collective-permute-start.9
  187.5 3.7 collective-permute-start.12
  189.7 4.3 collective-permute-start.13
  247.5 5.9 collective-permute-start.14
  248.8 5.8 collective-permute-start.15
  254.8 51.7 %collective-permute-start.16 = (f32[1,4,16]{2,1,0:T(4,128)S(1)}, f32[1,4,16]{2,1,0:T(4,128)S(1)}, u32[]{:S(2)}, u32[]{:S(2)}) collective-permute-start(f32[1,4,16]{2,1,0:T(4,128)S(1)} %fusion.138), channel_id=1, source_target_pairs={{4,0},{8,4},{12,8},{16,12},{20,16},{24,20},{28,24},{5,1},{9,5},{13... | collective-permute-start | bytes 776 | tf_op jit(solution)/shard_map/ppermute | solution.py:25
  256.1 50.4 %collective-permute-start.17 = (f32[1,4,16]{2,1,0:T(4,128)S(1)}, f32[1,4,16]{2,1,0:T(4,128)S(1)}, u32[]{:S(2)}, u32[]{:S(2)}) collective-permute-start(f32[1,4,16]{2,1,0:T(4,128)S(1)} %fusion.138), channel_id=1, source_target_pairs={{0,4},{4,8},{8,12},{12,16},{16,20},{20,24},{24,28},{1,5},{5,9},{9,... | collective-permute-start | bytes 776 | tf_op jit(solution)/shard_map/ppermute | solution.py:23
  306.6 60.8 %collective-permute-start.18 = (f32[1,4,16]{2,1,0:T(4,128)S(1)}, f32[1,4,16]{2,1,0:T(4,128)S(1)}, u32[]{:S(2)}, u32[]{:S(2)}) collective-permute-start(f32[1,4,16]{2,1,0:T(4,128)S(1)} %fusion.137), channel_id=1, source_target_pairs={{4,0},{8,4},{12,8},{16,12},{20,16},{24,20},{28,24},{5,1},{9,5},{13... | collective-permute-start | bytes 776 | tf_op jit(solution)/shard_map/ppermute | solution.py:25
  307.9 59.5 %collective-permute-start.19 = (f32[1,4,16]{2,1,0:T(4,128)S(1)}, f32[1,4,16]{2,1,0:T(4,128)S(1)}, u32[]{:S(2)}, u32[]{:S(2)}) collective-permute-start(f32[1,4,16]{2,1,0:T(4,128)S(1)} %fusion.137), channel_id=1, source_target_pairs={{0,4},{4,8},{8,12},{12,16},{16,20},{20,24},{24,28},{1,5},{5,9},{9,... | collective-permute-start | bytes 776 | tf_op jit(solution)/shard_map/ppermute | solution.py:23
  412.4 5.8 collective-permute-start.20
  416.8 5.5 collective-permute-start.21
  422.4 2.6 collective-permute-start.22
  423.7 3.6 collective-permute-start.23
  471.8 128.7 %copy-start.1 = (f32[8,8,128]{2,1,0:T(8,128)}, f32[8,8,128]{2,1,0:T(8,128)S(1)}, u32[]{:S(2)}) copy-start(f32[8,8,128]{2,1,0:T(8,128)S(1)} %get-tuple-element.16) | copy-start | bytes 98308
  478.6 6.2 collective-permute-start.24
  479.9 6.2 collective-permute-start.25
  486.3 52.3 %collective-permute-start.26 = (f32[1,4,16]{2,1,0:T(4,128)S(1)}, f32[1,4,16]{2,1,0:T(4,128)S(1)}, u32[]{:S(2)}, u32[]{:S(2)}) collective-permute-start(f32[1,4,16]{2,1,0:T(4,128)S(1)} %fusion.135), channel_id=1, source_target_pairs={{4,0},{8,4},{12,8},{16,12},{20,16},{24,20},{28,24},{5,1},{9,5},{13... | collective-permute-start | bytes 776 | tf_op jit(solution)/shard_map/ppermute | solution.py:25
  487.6 51.0 %collective-permute-start.27 = (f32[1,4,16]{2,1,0:T(4,128)S(1)}, f32[1,4,16]{2,1,0:T(4,128)S(1)}, u32[]{:S(2)}, u32[]{:S(2)}) collective-permute-start(f32[1,4,16]{2,1,0:T(4,128)S(1)} %fusion.135), channel_id=1, source_target_pairs={{0,4},{4,8},{8,12},{12,16},{16,20},{20,24},{24,28},{1,5},{5,9},{9,... | collective-permute-start | bytes 776 | tf_op jit(solution)/shard_map/ppermute | solution.py:23
  538.8 60.9 %collective-permute-start.28 = (f32[1,4,16]{2,1,0:T(4,128)S(1)}, f32[1,4,16]{2,1,0:T(4,128)S(1)}, u32[]{:S(2)}, u32[]{:S(2)}) collective-permute-start(f32[1,4,16]{2,1,0:T(4,128)S(1)} %fusion.134), channel_id=1, source_target_pairs={{4,0},{8,4},{12,8},{16,12},{20,16},{24,20},{28,24},{5,1},{9,5},{13... | collective-permute-start | bytes 776 | tf_op jit(solution)/shard_map/ppermute | solution.py:25
  540.1 59.6 %collective-permute-start.29 = (f32[1,4,16]{2,1,0:T(4,128)S(1)}, f32[1,4,16]{2,1,0:T(4,128)S(1)}, u32[]{:S(2)}, u32[]{:S(2)}) collective-permute-start(f32[1,4,16]{2,1,0:T(4,128)S(1)} %fusion.134), channel_id=1, source_target_pairs={{0,4},{4,8},{8,12},{12,16},{16,20},{20,24},{24,28},{1,5},{5,9},{9,... | collective-permute-start | bytes 776 | tf_op jit(solution)/shard_map/ppermute | solution.py:23
where the time goes:
time: 645 us; the launch traced here: 644 us
  local copies, waits for them, and re-layouts  308 us (48%)
  blocking collectives  194 us (30%)
  starting transfers between devices  84.2 us (13%)
  matrix products  24.9 us (4%)
  waiting for transfers between devices  14.7 us (2%)
  other arithmetic  10.2 us (2%)
  between operations  7.54 us (1%)
    gather x3, local copies, waits for them, and re-layouts, block_apply(): return product.reshape(cells)[places].reshape(shape)  137 us
    gather x3, local copies, waits for them, and re-layouts, block_apply(): residual.reshape(cells)[order].reshape(matrices.shape[0], matrices.shape[1])  137 us
    psum x3, blocking collectives, norm_of(): return lax.psum(jnp.sum(residual * smoothed), ('coarse', 'fine'))  125 us
    ppermute x15, starting transfers between devices, with_halo(): lax.ppermute(tail, axis, [(i, (i + 1) % count) for i in range(ends)])  64.9 us
    psum x1, blocking collectives, shards(): lax.psum(jnp.sum(search * operate_total), ('coarse', 'fine'))  42 us
    scatter x1, local copies, waits for them, and re-layouts, shards(): jnp.zeros((cells,), jnp.int32).at[order]  30.5 us
    dot_general x3, matrix products, block_apply(): jnp.einsum('bij,bj->bi', matrices, picked, precision=lax.Precision.HIGHEST)  24.9 us
    unnamed x3, blocking collectives  21.3 us
  transfers between devices with their start and end apart: 30, of which 7 were waited for; matrix products, arithmetic and copies ran while one was open for 52% of the time, Pallas kernels for 0%

commit v1 on v0

v1 whole, which is shorter than its diff:
```python
import functools

import jax
import jax.numpy as jnp
from jax import lax
from jax.experimental import pallas as pl
from jax.experimental.pallas import tpu as pltpu
from jax.sharding import PartitionSpec as P

ITERS = 2
SWEEPS = 4
omega = 0.8
restrict_scale = 0.25
MESH = pl.DeviceIdType.MESH
SUB = 8
LANES = 128
MAIN = 8
XLO, XHI, ZLO, ZHI, CORNER = 8, 9, 10, 11, 12
SLOTS = 13
DIRECTIONS = ((-1, 0), (1, 0), (0, -1), (0, 1), (-1, -1), (-1, 1), (1, -1), (1, 1))


def take(values, lanes):
    return jnp.take_along_axis(values, lanes, axis=1, mode="promise_in_bounds")


def full(row):
    return jnp.broadcast_to(row, (SUB, LANES))


def total_of(values):
    return jnp.sum(jnp.sum(values, axis=0, keepdims=True), axis=1, keepdims=True)


def kernel(
    owners, members, r_ref, cidx_ref, table_ref, cells_ref, inv_ref, amap_ref, diag_ref,
    x_out, r_out, p_out,
    mats, rot, key_in, lane_in, key_out, lane_out, moved,
    first_ext, first_cols, first_corner_src, first_corners,
    later_ext, later_cols, later_corner_src, later_corners,
    kap, amaps, w_ext, p_ext, r_cur, q_cur, kt, small,
    row_src, rows,
    mat_sems, send_sems, recv_sems, row_send, row_recv,
):
    count = owners * members
    o = lax.axis_index("coarse")
    m = lax.axis_index("fine")
    me = o * members + m
    groups = cells_ref.shape[0]
    sub = lax.broadcasted_iota(jnp.int32, (SUB, LANES), 0)
    lane = lax.broadcasted_iota(jnp.int32, (SUB, LANES), 1)
    zero = jnp.zeros((SUB, LANES), jnp.float32)

    mat_copies = [
        pltpu.make_async_copy(
            inv_ref.at[pl.ds(u * SUB, SUB)], mats.at[pl.ds(u * SUB, SUB)], mat_sems.at[u]
        )
        for u in range(groups)
    ]
    for copy in mat_copies:
        copy.start()

    for slot in range(MAIN, CORNER):
        for f in range(3):
            first_ext[slot, f] = zero
        later_ext[slot, 0] = zero
    for c in range(4):
        first_corners[c] = zero
        later_corners[c] = zero

    barrier = pltpu.get_barrier_semaphore()

    def other(d):
        t = lax.rem(me + d, count)
        return {"coarse": lax.div(t, members), "fine": lax.rem(t, members)}

    def announce(d, carry):
        pl.semaphore_signal(barrier, inc=1, device_id=other(d), device_id_type=MESH)
        return carry

    lax.fori_loop(1, count, announce, 0)

    def keys_of(source):
        row = lax.shift_right_logical(source, 7)
        turn = (jnp.bitwise_and(row, 7) - sub) & 7
        return jnp.bitwise_and(row, ~7) + turn, jnp.bitwise_and(source, 127)

    for g in range(groups):
        key, lanes = keys_of(cells_ref[g])
        key_in[g] = key
        lane_in[g] = lanes

    def load_turns(values):
        for g in range(len(values)):
            for turn in range(SUB):
                rot[g * SUB + turn] = (
                    values[g] if turn == 0 else pltpu.roll(values[g], SUB - turn, 0)
                )

    def permuted(key, lanes):
        parts = [zero, zero]
        for k in range(groups * SUB):
            parts[k % 2] = jnp.where(key == k, take(rot[k], lanes), parts[k % 2])
        return parts[0] + parts[1]

    tall = lax.broadcasted_iota(jnp.int32, (groups * SUB, LANES), 0)
    taller = lax.broadcasted_iota(jnp.int32, (LANES, LANES), 0)
    wide = lax.broadcasted_iota(jnp.int32, (groups * SUB, LANES), 1).astype(jnp.float32)

    def find(g, carry):
        block = cells_ref[g]
        for b in range(SUB):
            source = block[b : b + 1, :]
            hit = tall == jnp.broadcast_to(lax.shift_right_logical(source, 7), tall.shape)
            number = (g * SUB + b).astype(jnp.float32)
            left = jnp.concatenate(
                [jnp.where(hit, number, 0.0), jnp.where(hit, wide, 0.0)], axis=0
            ).astype(jnp.bfloat16)
            right = jnp.where(
                taller == jnp.broadcast_to(jnp.bitwise_and(source, 127), taller.shape), 1.0, 0.0
            ).astype(jnp.bfloat16)
            carry = carry + lax.dot_general(
                left, right, (((1,), (1,)), ((), ())), preferred_element_type=jnp.float32
            )
        return carry

    found = lax.fori_loop(
        0, groups, find, jnp.zeros((2 * groups * SUB, LANES), jnp.float32)
    ).astype(jnp.int32)
    for g in range(groups):
        block = found[g * SUB : (g + 1) * SUB]
        place = found[(groups + g) * SUB : (groups + g + 1) * SUB]
        key, lanes = keys_of(block * LANES + place)
        key_out[g] = key
        lane_out[g] = lanes

    small[...] = jnp.zeros(small.shape, jnp.float32)
    small[0, 0:1, 0 : table_ref.shape[1]] = table_ref[...]
    small[1, 0:1, 0 : diag_ref.shape[2]] = diag_ref[0]
    boxes = diag_ref.shape[2]
    table = full(small[0, 0:1, :])
    for x in range(MAIN):
        first_ext[x, 1] = take(table, cidx_ref[x])
        first_ext[x, 2] = (amap_ref[x] + 1).astype(jnp.float32)
        amaps[x] = amap_ref[x]

    spread_sub = lax.shift_right_logical(lane, 4)
    spread_key = (spread_sub - sub) & 7
    spread_lane = (lane & 15) * 8 + sub

    def block_apply(values, done_with_dot):
        load_turns(values)

        def one(u, dot):
            picked = permuted(key_in[u], lane_in[u])
            columns = zero
            for turn in range(SUB):
                turned = picked if turn == 0 else pltpu.roll(picked, SUB - turn, 0)
                columns = jnp.where(spread_key == turn, take(turned, spread_lane), columns)
            product = zero
            for b in range(SUB):
                parts = [None, None]
                for j in range(LANES // SUB):
                    at = b * (LANES // SUB) + j
                    term = mats[u * SUB + b, pl.ds(j * SUB, SUB), :] * jnp.broadcast_to(
                        columns[:, at : at + 1], (SUB, LANES)
                    )
                    parts[j % 2] = term if parts[j % 2] is None else parts[j % 2] + term
                line = jnp.sum(parts[0] + parts[1], axis=0, keepdims=True)
                product = jnp.where(sub == b, full(line), product)
            moved[u] = product
            return dot + picked * product

        dot = lax.fori_loop(0, groups, one, zero)
        done_with_dot(total_of(dot))
        load_turns([moved[g] for g in range(groups)])

        def back(g, carry):
            moved[g] = permuted(key_out[g], lane_out[g])
            return carry

        lax.fori_loop(0, groups, back, 0)
        return [moved[g] for g in range(groups)]

    base = lax.shift_right_logical(lane, 3)

    def restrict(values):
        sums = []
        for move in (-1, 0, 1):
            total = zero
            for x in range(MAIN):
                total = total + jnp.where(amaps[x] - base == move, values[x], 0.0)
            sums.append(total)
        total = pltpu.roll(sums[0], LANES - SUB, 1) + sums[1] + pltpu.roll(sums[2], SUB, 1)
        total = full(jnp.sum(total, axis=0, keepdims=True))
        for step in (1, 2, 4):
            total = total + pltpu.roll(total, LANES - step, 1)
        return jnp.where(lane < boxes, restrict_scale * take(total, (lane * SUB) & 127), 0.0)

    def row_copy(index, src, dst, device):
        return pltpu.make_async_remote_copy(
            src_ref=src, dst_ref=dst, send_sem=row_send.at[index], recv_sem=row_recv.at[index],
            device_id=device, device_id_type=MESH,
        )

    def send_rows(index, row):
        row_src[index] = row[0:1, :]
        rows[index, me] = row[0:1, :]

        def one(d, carry):
            row_copy(index, row_src.at[index], rows.at[index, me], other(d)).start()
            return carry

        lax.fori_loop(1, count, one, 0)

    def wait_rows(index):
        part = rows.at[index, pl.ds(0, count - 1)]
        both = row_copy(index, part, part, other(1))
        both.wait_send()
        both.wait_recv()
        return rows[index].reshape(count, LANES)

    def scalar(row, number):
        at = 2 * boxes + number
        return row[:, at : at + 1]

    def with_scalar(row, number, value):
        return jnp.where(lane == 2 * boxes + number, full(value), row)

    def edge_rows(values, z):
        result = zero
        for x in range(MAIN):
            result = jnp.where(sub == x, full(values[x][z : z + 1, :]), result)
        return result

    def halo_copies(ring, ext, cols, corner_src, corners):
        copies = []
        for number, (do, dm) in enumerate(DIRECTIONS):
            if dm == 0:
                src = ext.at[MAIN - 1 if do == 1 else 0]
                dst = ext.at[XLO if do == 1 else XHI]
            elif do == 0:
                src = cols.at[1 if dm == 1 else 0]
                dst = ext.at[ZLO if dm == 1 else ZHI]
            else:
                at = 2 * (0 if do == 1 else 1) + (0 if dm == 1 else 1)
                src = corner_src.at[at]
                dst = corners.at[at]
            to_o, to_m = o + do, m + dm
            from_o, from_m = o - do, m - dm
            goes = (to_o >= 0) & (to_o < owners) & (to_m >= 0) & (to_m < members)
            comes = (from_o >= 0) & (from_o < owners) & (from_m >= 0) & (from_m < members)
            copies.append(
                (
                    goes,
                    comes,
                    pltpu.make_async_remote_copy(
                        src_ref=src, dst_ref=dst,
                        send_sem=send_sems.at[ring, number], recv_sem=recv_sems.at[ring, number],
                        device_id={"coarse": to_o, "fine": to_m}, device_id_type=MESH,
                    ),
                )
            )
        return copies

    def start_halo(ring, fields, ext, cols, corner_src, corners):
        packs = [zero, zero, zero, zero]
        for f, values in enumerate(fields):
            cols[0, f] = edge_rows(values, 0)
            cols[1, f] = edge_rows(values, SUB - 1)
            for side_x in range(2):
                for side_z in range(2):
                    at = 2 * side_x + side_z
                    x = MAIN - 1 if side_x == 0 else 0
                    z = SUB - 1 if side_z == 0 else 0
                    packs[at] = jnp.where(sub == f, full(values[x][z : z + 1, :]), packs[at])
        for at in range(4):
            corner_src[at] = packs[at]
        copies = halo_copies(ring, ext, cols, corner_src, corners)
        for goes, _, copy in copies:
            pl.when(goes)(copy.start)
        return copies

    def wait_halo(copies):
        for goes, comes, copy in copies:
            pl.when(goes)(copy.wait_send)
            pl.when(comes)(copy.wait_recv)

    def corner_rows(corners, f):
        result = zero
        for at in range(4):
            result = jnp.where(sub == at, full(corners[at][f : f + 1, :]), result)
        return result

    def shifted(values, low, high):
        before = jnp.where(sub == 0, full(low), pltpu.roll(values, 1, 0))
        after = jnp.where(sub == SUB - 1, full(high), pltpu.roll(values, SUB - 1, 0))
        return values + 0.5 * (before + after)

    def smear(v):
        planes = [v[XLO]] + [v[x] for x in range(MAIN)] + [v[XHI]]
        corner = v[CORNER]
        low = shifted(v[ZLO], corner[0:1, :], corner[2:3, :])
        high = shifted(v[ZHI], corner[1:2, :], corner[3:4, :])
        result = []
        for x in range(MAIN):
            mid = planes[x + 1] + 0.5 * (planes[x] + planes[x + 2])
            mid = shifted(mid, low[x : x + 1, :], high[x : x + 1, :])
            before = jnp.where(lane == 0, 0.0, pltpu.roll(mid, 1, 1))
            after = jnp.where(lane == LANES - 1, 0.0, pltpu.roll(mid, LANES - 1, 1))
            result.append(mid + 0.5 * (before + after))
        return result

    node = lax.broadcasted_iota(jnp.int32, (count, LANES), 0)
    node_lane = lax.broadcasted_iota(jnp.int32, (count, LANES), 1)
    member = lax.rem(node, members)

    def coarse_solve(source, inverse):
        guess = omega * source * inverse
        for sweep in range(SWEEPS - 1):
            beside = pltpu.roll(guess, 1, 1) + pltpu.roll(guess, LANES - 1, 1)
            beside = beside + jnp.where(member == 0, 0.0, pltpu.roll(guess, 1, 0))
            beside = beside + jnp.where(
                member == members - 1, 0.0, pltpu.roll(guess, count - 1, 0)
            )
            beside = beside + jnp.where(node < members, 0.0, pltpu.roll(guess, members, 0))
            beside = beside + jnp.where(
                node >= count - members, 0.0, pltpu.roll(guess, count - members, 0)
            )
            guess = (1.0 - omega) * guess + omega * (source + beside) * inverse
        return guess

    def prolonged(guess, slot_row):
        return slot_row

    start = [r_ref[x] for x in range(MAIN)]
    first_row = restrict(start) + pltpu.roll(full(small[1, 0:1, :]), boxes, 1)
    for copy in mat_copies:
        copy.wait()

    def first_send(dot):
        pl.semaphore_wait(barrier, count - 1)
        send_rows(0, with_scalar(first_row, 0, dot))

    w = block_apply(start, first_send)
    for x in range(MAIN):
        first_ext[x, 0] = w[x]
    kappas = [first_ext[x, 1] for x in range(MAIN)]
    maps = [first_ext[x, 2] for x in range(MAIN)]
    copies = start_halo(
        0, [w, kappas, maps], first_ext, first_cols, first_corner_src, first_corners
    )
    gathered = wait_rows(0)
    diagonal = pltpu.roll(gathered, LANES - boxes, 1)
    inverse = jnp.where(
        node_lane < boxes, 1.0 / jnp.where(node_lane < boxes, 6.0 + diagonal, 1.0), 0.0
    )
    source = jnp.where(node_lane < boxes, gathered, 0.0)
    guess = coarse_solve(source, inverse)
    local_part = scalar(jnp.sum(gathered, axis=0, keepdims=True), 0)
    norm = local_part + total_of(source * guess) * (1.0 / restrict_scale)
    solved = small.shape[0]

    def guess_rows(guess):
        picks = {}
        for do in (-1, 0, 1):
            for dm in (-1, 0, 1):
                wanted = me + do * members + dm
                picks[(do, dm)] = full(
                    jnp.sum(jnp.where(node == wanted, guess, 0.0), axis=0, keepdims=True)
                )
        return picks

    def add_coarse(values, guess):
        picks = guess_rows(guess)
        result = []
        for x in range(MAIN):
            result.append(values[x] + take(picks[(0, 0)], amaps[x]))
        for slot, way in ((XLO, (-1, 0)), (XHI, (1, 0)), (ZLO, (0, -1)), (ZHI, (0, 1))):
            result.append(values[slot] + take(picks[way], amaps[slot]))
        corner = zero
        for at, way in enumerate(((-1, -1), (-1, 1), (1, -1), (1, 1))):
            corner = jnp.where(sub == at, take(picks[way], amaps[CORNER]), corner)
        result.append(values[CORNER] + corner)
        return result

    wait_halo(copies)
    for slot in range(SLOTS):
        if slot == CORNER:
            parts = [corner_rows(first_corners, f) for f in range(3)]
        else:
            parts = [first_ext[slot, f] for f in range(3)]
        w_ext[slot] = parts[0]
        kap[slot] = parts[1]
        if slot >= MAIN:
            amaps[slot] = (parts[2].astype(jnp.int32) + (LANES - 1)) & (LANES - 1)
    smeared = smear([kap[s] for s in range(SLOTS)])
    for x in range(MAIN):
        kt[x] = 8.0 * kap[x] + smeared[x]
        r_cur[x] = r_ref[x]
    z = add_coarse([w_ext[s] for s in range(SLOTS)], guess)
    for slot in range(SLOTS):
        p_ext[slot] = z[slot]

    for step in range(ITERS):
        last = step == ITERS - 1
        p = [p_ext[s] for s in range(SLOTS)]
        flat = smear(p)
        steep = smear([p[s] * kap[s] for s in range(SLOTS)])
        along, across = zero, zero
        for x in range(MAIN):
            q = p[x] * kt[x] - kap[x] * flat[x] - steep[x]
            q_cur[x] = q
            along = along + p[x] * q
            across = across + w_ext[x] * q
        image = [q_cur[x] for x in range(MAIN)]
        row = restrict(image)
        row = with_scalar(row, 0, total_of(along))
        row = with_scalar(row, 1, total_of(across))

        def later_send(dot, row=row, step=step):
            send_rows(1 + step, with_scalar(row, 2, dot))

        bq = block_apply(image, later_send)
        if not last:
            for x in range(MAIN):
                later_ext[x, 0] = bq[x]
            copies = start_halo(
                1 + step, [bq], later_ext, later_cols, later_corner_src, later_corners
            )
        gathered = wait_rows(1 + step)
        sums = jnp.sum(gathered, axis=0, keepdims=True)
        alpha = norm / scalar(sums, 0)
        source = source - alpha * jnp.where(node_lane < boxes, gathered, 0.0)
        guess = coarse_solve(source, inverse)
        local_part = (
            local_part - 2.0 * alpha * scalar(sums, 1) + alpha * alpha * scalar(sums, 2)
        )
        following = local_part + total_of(source * guess) * (1.0 / restrict_scale)
        beta = full(following / norm)
        alpha = full(alpha)
        norm = following
        for x in range(MAIN):
            moved_x = alpha * p_ext[x]
            x_out[x] = moved_x if step == 0 else x_out[x] + moved_x
            r_cur[x] = r_cur[x] - alpha * q_cur[x]
        if not last:
            wait_halo(copies)
            change = [later_ext[s, 0] for s in range(CORNER)] + [corner_rows(later_corners, 0)]
            for slot in range(SLOTS):
                w_ext[slot] = w_ext[slot] - alpha * change[slot]
            z = add_coarse([w_ext[s] for s in range(SLOTS)], guess)
            for slot in range(SLOTS):
                p_ext[slot] = z[slot] + beta * p_ext[slot]
        else:
            own = full(jnp.sum(jnp.where(node == me, guess, 0.0), axis=0, keepdims=True))
            for x in range(MAIN):
                z_x = w_ext[x] - alpha * bq[x] + take(own, amaps[x])
                p_out[x] = z_x + beta * p_ext[x]
                r_out[x] = r_cur[x]


def shards(
    owners, members, right_side, coefficient_index, material_coefficients, block_cells,
    block_inverses, aggregate_map, coarse_diagonal,
):
    blocks, side = block_cells.shape[2], block_cells.shape[3]
    assert right_side.shape == (SUB, SUB, LANES) and side == LANES and blocks == SUB * SUB
    count = owners * members
    groups = blocks // SUB
    field = jax.ShapeDtypeStruct(right_side.shape, jnp.float32)
    vmem = pl.BlockSpec(memory_space=pltpu.VMEM)
    f32, i32 = jnp.float32, jnp.int32
    tile = (SUB, LANES)
    return pl.pallas_call(
        functools.partial(kernel, owners, members),
        out_shape=(field, field, field),
        in_specs=[vmem, vmem, vmem, vmem, pl.BlockSpec(memory_space=pl.ANY), vmem, vmem],
        out_specs=(vmem, vmem, vmem),
        scratch_shapes=[
            pltpu.VMEM((blocks, side, side), f32),
            pltpu.VMEM((blocks,) + tile, f32),
            pltpu.VMEM((groups,) + tile, i32),
            pltpu.VMEM((groups,) + tile, i32),
            pltpu.VMEM((groups,) + tile, i32),
            pltpu.VMEM((groups,) + tile, i32),
            pltpu.VMEM((groups,) + tile, f32),
            pltpu.VMEM((CORNER, 3) + tile, f32),
            pltpu.VMEM((2, 3) + tile, f32),
            pltpu.VMEM((4,) + tile, f32),
            pltpu.VMEM((4,) + tile, f32),
            pltpu.VMEM((CORNER, 1) + tile, f32),
            pltpu.VMEM((2, 1) + tile, f32),
            pltpu.VMEM((4,) + tile, f32),
            pltpu.VMEM((4,) + tile, f32),
            pltpu.VMEM((SLOTS,) + tile, f32),
            pltpu.VMEM((SLOTS,) + tile, i32),
            pltpu.VMEM((SLOTS,) + tile, f32),
            pltpu.VMEM((SLOTS,) + tile, f32),
            pltpu.VMEM((MAIN,) + tile, f32),
            pltpu.VMEM((MAIN,) + tile, f32),
            pltpu.VMEM((MAIN,) + tile, f32),
            pltpu.VMEM((2,) + tile, f32),
            pltpu.VMEM((1 + ITERS, 1, LANES), f32),
            pltpu.VMEM((1 + ITERS, count, 1, LANES), f32),
            pltpu.SemaphoreType.DMA((groups,)),
            pltpu.SemaphoreType.DMA((ITERS, len(DIRECTIONS))),
            pltpu.SemaphoreType.DMA((ITERS, len(DIRECTIONS))),
            pltpu.SemaphoreType.DMA((1 + ITERS,)),
            pltpu.SemaphoreType.DMA((1 + ITERS,)),
        ],
        compiler_params=pltpu.CompilerParams(
            collective_id=0, has_side_effects=True, vmem_limit_bytes=32 << 20
        ),
    )(
        right_side,
        coefficient_index,
        material_coefficients.reshape(1, -1),
        block_cells.reshape(groups, SUB, LANES),
        block_inverses.reshape(blocks, side, side),
        aggregate_map,
        coarse_diagonal,
    )


def solution(mesh):
    three = P("coarse", "fine", None)
    return jax.shard_map(
        functools.partial(shards, mesh.shape["coarse"], mesh.shape["fine"]),
        mesh=mesh,
        in_specs=(
            three,
            three,
            P(),
            P("coarse", "fine", None, None),
            P("coarse", "fine", None, None, None),
            three,
            three,
        ),
        out_specs=(three, three, three),
        check_vma=False,
    )
```

time: 645 us -> 46.2 us (0.07)
  local copies, waits for them, and re-layouts: 308 us -> 8.37 us
  blocking collectives: 194 us -> 0 us
  starting transfers between devices: 84.2 us -> 0 us
  Pallas kernels: 0 us -> 36.7 us
  matrix products: 24.9 us -> 0 us
  waiting for transfers between devices: 14.7 us -> 0 us
  other arithmetic: 10.2 us -> 0 us
  between operations: 7.54 us -> 0.66 us
    gather x6 -> x0, local copies, waits for them, and re-layouts: 273 us -> none  [the longest x3 137 us: block_apply(): return product.reshape(cells)[places].reshape(shape)]
    psum x4 -> x0, blocking collectives: 167 us -> none  [the longest x3 125 us: norm_of(): return lax.psum(jnp.sum(residual * smoothed), ('coarse', 'fine'))]
    ppermute x30 -> x0, starting transfers between devices: 84.2 us -> none  [the longest x15 64.9 us: with_halo(): lax.ppermute(tail, axis, [(i, (i + 1) % count) for i in range(ends)])]
    pallas_call x0 -> x1, Pallas kernels: none -> 36.7 us  [shards(): pl.pallas_call(functools.partial(kernel, owners, members), out_shape=(fie...]
    scatter x1 -> x0, local copies, waits for them, and re-layouts: 30.5 us -> none  [shards(): jnp.zeros((cells,), jnp.int32).at[order]]
    dot_general x3 -> x0, matrix products: 24.9 us -> none  [block_apply(): jnp.einsum('bij,bj->bi', matrices, picked, precision=lax.Precision.HIGHEST)]
    unnamed x3 -> x0, blocking collectives: 21.3 us -> none
    ppermute x30 -> x0, waiting for transfers between devices: 14.7 us -> none  [the longest x15 10.9 us: with_halo(): lax.ppermute(head, axis, [((i + 1) % count, i) for i in range(ends)])]
  transfers between devices with their start and end apart: 30 -> 0, of which waited for: 7 -> 0; matrix products, arithmetic and copies ran while one was open for 52% -> 0% of each run, Pallas kernels for 0% -> 0%
where the time goes in v1:
time: 46.2 us; the launch traced here: 45.8 us
  Pallas kernels  36.7 us (79%)
  local copies, waits for them, and re-layouts  8.37 us (18%)
  between operations  0.66 us (1%)
    pallas_call x1, Pallas kernels, shards(): pl.pallas_call(functools.partial(kernel, owners, members), out_shape=(fie...  36.7 us
    unnamed x17, local copies, waits for them, and re-layouts  8.37 us

profile of v1, /device:TPU:0, one launch (start us, length us, event | category | flops | bytes accessed | tf_op | source)
XLA Modules:
  0.0 45.8 jit_solution(7510271065076328452)
XLA Ops:
  0.6 0.0 copy-start
  0.6 2.2 %copy-done = f32[1,1,64,128,128]{4,3,2,1,0:T(8,128)S(1)} copy-done((f32[1,1,64,128,128]{4,3,2,1,0:T(8,128)S(1)}, f32[1,1,64,128,128]{4,3,2,1,0:T(8,128)}, u32[]{:S(2)}) %copy-start) | copy-done | bytes 4194328
  2.8 0.0 copy-start.1
  2.8 0.8 %copy-done.1 = f32[8,8,128]{2,1,0:T(8,128)S(1)} copy-done((f32[8,8,128]{2,1,0:T(8,128)S(1)}, f32[8,8,128]{2,1,0:T(8,128)}, u32[]{:S(2)}) %copy-start.1) | copy-done | bytes 32792
  3.6 0.0 copy-start.2
  3.6 0.8 %copy-done.2 = s32[8,8,128]{2,1,0:T(8,128)S(1)} copy-done((s32[8,8,128]{2,1,0:T(8,128)S(1)}, s32[8,8,128]{2,1,0:T(8,128)}, u32[]{:S(2)}) %copy-start.2) | copy-done | bytes 32792
  4.3 0.0 copy-start.3
  4.3 0.8 %copy-done.3 = s32[1,1,64,128]{3,2,1,0:T(8,128)S(1)} copy-done((s32[1,1,64,128]{3,2,1,0:T(8,128)S(1)}, s32[1,1,64,128]{3,2,1,0:T(8,128)}, u32[]{:S(2)}) %copy-start.3) | copy-done | bytes 32792
  5.1 0.0 copy-start.4
  5.1 0.8 %copy-done.4 = s32[8,8,128]{2,1,0:T(8,128)S(1)} copy-done((s32[8,8,128]{2,1,0:T(8,128)S(1)}, s32[8,8,128]{2,1,0:T(8,128)}, u32[]{:S(2)}) %copy-start.4) | copy-done | bytes 32792
  5.9 0.0 copy-start.5
  5.9 0.7 %copy-done.5 = f32[16]{0:T(128)S(1)} copy-done((f32[16]{0:T(128)S(1)}, f32[16]{0:T(128)}, u32[]{:S(2)}) %copy-start.5) | copy-done | bytes 88
  6.5 0.0 copy-start.6
  6.5 0.7 %copy-done.6 = f32[1,1,16]{2,1,0:T(1,128)S(1)} copy-done((f32[1,1,16]{2,1,0:T(1,128)S(1)}, f32[1,1,16]{2,1,0:T(1,128)}, u32[]{:S(2)}) %copy-start.6) | copy-done | bytes 88
  7.2 36.7 %shard_map.94 = (f32[8,8,128]{2,1,0:T(8,128)S(1)}, f32[8,8,128]{2,1,0:T(8,128)S(1)}, f32[8,8,128]{2,1,0:T(8,128)S(1)}) custom-call(f32[8,8,128]{2,1,0:T(8,128)S(1)} %copy-done.1, s32[8,8,128]{2,1,0:T(8,128)S(1)} %copy-done.2, f32[1,16]{1,0:T(1,128)S(1)} %bitcast.5, s32[8,8,128]{2,1,0:T(8,128)S(1)} %bitcast.4, f32[64,128,128]{2,1,0:T(8,128)S(1)} %bitcast.3, ...), custom_call_target="tpu_custom_call" | custom-call | tf_op jit(solution)/shard_map/pallas_call | solution.py:475
  43.9 0.6 %copy.13 = f32[8,8,128]{2,1,0:T(8,128)} copy(f32[8,8,128]{2,1,0:T(8,128)S(1)} %get-tuple-element.6) | data formatting | bytes 65536
  44.5 0.6 %copy.14 = f32[8,8,128]{2,1,0:T(8,128)} copy(f32[8,8,128]{2,1,0:T(8,128)S(1)} %get-tuple-element.7) | data formatting | bytes 65536
  45.1 0.6 %copy.15 = f32[8,8,128]{2,1,0:T(8,128)} copy(f32[8,8,128]{2,1,0:T(8,128)S(1)} %get-tuple-element.8) | data formatting | bytes 65536
Async XLA Ops:
  0.6 2.2 %copy-start = (f32[1,1,64,128,128]{4,3,2,1,0:T(8,128)S(1)}, f32[1,1,64,128,128]{4,3,2,1,0:T(8,128)}, u32[]{:S(2)}) copy-start(f32[1,1,64,128,128]{4,3,2,1,0:T(8,128)} %param.11) | copy-start | bytes 12582916
  2.8 0.8 %copy-start.1 = (f32[8,8,128]{2,1,0:T(8,128)S(1)}, f32[8,8,128]{2,1,0:T(8,128)}, u32[]{:S(2)}) copy-start(f32[8,8,128]{2,1,0:T(8,128)} %r_ref.1) | copy-start | bytes 98308
  3.6 0.8 %copy-start.2 = (s32[8,8,128]{2,1,0:T(8,128)S(1)}, s32[8,8,128]{2,1,0:T(8,128)}, u32[]{:S(2)}) copy-start(s32[8,8,128]{2,1,0:T(8,128)} %cidx_ref.1) | copy-start | bytes 98308
  4.3 0.8 %copy-start.3 = (s32[1,1,64,128]{3,2,1,0:T(8,128)S(1)}, s32[1,1,64,128]{3,2,1,0:T(8,128)}, u32[]{:S(2)}) copy-start(s32[1,1,64,128]{3,2,1,0:T(8,128)} %param.10) | copy-start | bytes 98308
  5.1 0.8 %copy-start.4 = (s32[8,8,128]{2,1,0:T(8,128)S(1)}, s32[8,8,128]{2,1,0:T(8,128)}, u32[]{:S(2)}) copy-start(s32[8,8,128]{2,1,0:T(8,128)} %amap_ref.1) | copy-start | bytes 98308
  5.9 0.7 %copy-start.5 = (f32[16]{0:T(128)S(1)}, f32[16]{0:T(128)}, u32[]{:S(2)}) copy-start(f32[16]{0:T(128)} %param.9) | copy-start | bytes 196
  6.5 0.7 %copy-start.6 = (f32[1,1,16]{2,1,0:T(1,128)S(1)}, f32[1,1,16]{2,1,0:T(1,128)}, u32[]{:S(2)}) copy-start(f32[1,1,16]{2,1,0:T(1,128)} %diag_ref.1) | copy-start | bytes 196

commit v2 on v1

--- a/solution.py
+++ b/solution.py
@@ -33,9 +33,10 @@
 
 
 def kernel(
-    owners, members, r_ref, cidx_ref, table_ref, cells_ref, inv_ref, amap_ref, diag_ref,
+    owners, members, r_hbm, cidx_hbm, table_hbm, cells_hbm, inv_ref, amap_hbm, diag_hbm,
     x_out, r_out, p_out,
-    mats, rot, key_in, lane_in, key_out, lane_out, moved,
+    r_ref, cidx_ref, table_ref, cells_ref, amap_ref, diag_ref, in_sems,
+    mats, halves, rot, key_in, lane_in, key_out, lane_out, moved,
     first_ext, first_cols, first_corner_src, first_corners,
     later_ext, later_cols, later_corner_src, later_corners,
     kap, amaps, w_ext, p_ext, r_cur, q_cur, kt, small,
@@ -51,14 +52,27 @@
     lane = lax.broadcasted_iota(jnp.int32, (SUB, LANES), 1)
     zero = jnp.zeros((SUB, LANES), jnp.float32)
 
-    mat_copies = [
-        pltpu.make_async_copy(
-            inv_ref.at[pl.ds(u * SUB, SUB)], mats.at[pl.ds(u * SUB, SUB)], mat_sems.at[u]
+    in_copies = [
+        pltpu.make_async_copy(src, dst, in_sems.at[at])
+        for at, (src, dst) in enumerate(
+            (
+                (cells_hbm, cells_ref),
+                (r_hbm, r_ref),
+                (amap_hbm, amap_ref),
+                (cidx_hbm, cidx_ref),
+                (table_hbm, table_ref),
+                (diag_hbm, diag_ref),
+            )
         )
-        for u in range(groups)
     ]
-    for copy in mat_copies:
+    for copy in in_copies:
         copy.start()
+    def mat_copy(u):
+        part = pl.ds(u * SUB, SUB)
+        return pltpu.make_async_copy(inv_ref.at[part], mats.at[part], mat_sems.at[u])
+
+    for u in range(groups):
+        mat_copy(u).start()
 
     for slot in range(MAIN, CORNER):
         for f in range(3):
@@ -79,6 +93,8 @@
         return carry
 
     lax.fori_loop(1, count, announce, 0)
+
+    in_copies[0].wait()
 
     def keys_of(source):
         row = lax.shift_right_logical(source, 7)
@@ -134,6 +150,8 @@
         key_out[g] = key
         lane_out[g] = lanes
 
+    for copy in in_copies[1:]:
+        copy.wait()
     small[...] = jnp.zeros(small.shape, jnp.float32)
     small[0, 0:1, 0 : table_ref.shape[1]] = table_ref[...]
     small[1, 0:1, 0 : diag_ref.shape[2]] = diag_ref[0]
@@ -144,30 +162,29 @@
         first_ext[x, 2] = (amap_ref[x] + 1).astype(jnp.float32)
         amaps[x] = amap_ref[x]
 
-    spread_sub = lax.shift_right_logical(lane, 4)
-    spread_key = (spread_sub - sub) & 7
-    spread_lane = (lane & 15) * 8 + sub
-
-    def block_apply(values, done_with_dot):
+    def split(values):
+        high = values.astype(jnp.bfloat16)
+        low = (values - high.astype(jnp.float32)).astype(jnp.bfloat16)
+        return high, low
+
+    def block_apply(values, done_with_dot, first=False):
         load_turns(values)
 
         def one(u, dot):
+            if first:
+                mat_copy(u).wait()
+                for b in range(SUB):
+                    high, low = split(mats[u * SUB + b])
+                    halves[u * SUB + b, :, 0:LANES] = high
+                    halves[u * SUB + b, :, LANES : 2 * LANES] = low
             picked = permuted(key_in[u], lane_in[u])
-            columns = zero
-            for turn in range(SUB):
-                turned = picked if turn == 0 else pltpu.roll(picked, SUB - turn, 0)
-                columns = jnp.where(spread_key == turn, take(turned, spread_lane), columns)
+            left = jnp.concatenate(split(picked), axis=0)
             product = zero
             for b in range(SUB):
-                parts = [None, None]
-                for j in range(LANES // SUB):
-                    at = b * (LANES // SUB) + j
-                    term = mats[u * SUB + b, pl.ds(j * SUB, SUB), :] * jnp.broadcast_to(
-                        columns[:, at : at + 1], (SUB, LANES)
-                    )
-                    parts[j % 2] = term if parts[j % 2] is None else parts[j % 2] + term
-                line = jnp.sum(parts[0] + parts[1], axis=0, keepdims=True)
-                product = jnp.where(sub == b, full(line), product)
+                both = jnp.dot(left, halves[u * SUB + b], preferred_element_type=jnp.float32)
+                line = both[:SUB, :LANES] + (both[SUB:, :LANES] + both[:SUB, LANES:])
+                line = line + both[SUB:, LANES:]
+                product = jnp.where(sub == b, line, product)
             moved[u] = product
             return dot + picked * product
 
@@ -330,19 +347,14 @@
             guess = (1.0 - omega) * guess + omega * (source + beside) * inverse
         return guess
 
-    def prolonged(guess, slot_row):
-        return slot_row
-
     start = [r_ref[x] for x in range(MAIN)]
     first_row = restrict(start) + pltpu.roll(full(small[1, 0:1, :]), boxes, 1)
-    for copy in mat_copies:
-        copy.wait()
 
     def first_send(dot):
         pl.semaphore_wait(barrier, count - 1)
         send_rows(0, with_scalar(first_row, 0, dot))
 
-    w = block_apply(start, first_send)
+    w = block_apply(start, first_send, True)
     for x in range(MAIN):
         first_ext[x, 0] = w[x]
     kappas = [first_ext[x, 1] for x in range(MAIN)]
@@ -359,7 +371,6 @@
     guess = coarse_solve(source, inverse)
     local_part = scalar(jnp.sum(gathered, axis=0, keepdims=True), 0)
     norm = local_part + total_of(source * guess) * (1.0 / restrict_scale)
-    solved = small.shape[0]
 
     def guess_rows(guess):
         picks = {}
@@ -460,6 +471,15 @@
                 r_out[x] = r_cur[x]
 
 
+def emit(x_ref, r_ref, p_ref, x_out, r_out, p_out, sems):
+    pairs = ((x_ref, x_out), (r_ref, r_out), (p_ref, p_out))
+    copies = [pltpu.make_async_copy(a, b, sems.at[i]) for i, (a, b) in enumerate(pairs)]
+    for copy in copies:
+        copy.start()
+    for copy in copies:
+        copy.wait()
+
+
 def shards(
     owners, members, right_side, coefficient_index, material_coefficients, block_cells,
     block_inverses, aggregate_map, coarse_diagonal,
@@ -472,13 +492,22 @@
     vmem = pl.BlockSpec(memory_space=pltpu.VMEM)
     f32, i32 = jnp.float32, jnp.int32
     tile = (SUB, LANES)
-    return pl.pallas_call(
+    hbm = pl.BlockSpec(memory_space=pltpu.HBM)
+    results = pl.pallas_call(
         functools.partial(kernel, owners, members),
         out_shape=(field, field, field),
-        in_specs=[vmem, vmem, vmem, vmem, pl.BlockSpec(memory_space=pl.ANY), vmem, vmem],
+        in_specs=[hbm] * 7,
         out_specs=(vmem, vmem, vmem),
         scratch_shapes=[
+            pltpu.VMEM(right_side.shape, f32),
+            pltpu.VMEM(right_side.shape, i32),
+            pltpu.VMEM((1,) + material_coefficients.shape, f32),
+            pltpu.VMEM((groups,) + tile, i32),
+            pltpu.VMEM(right_side.shape, i32),
+            pltpu.VMEM(coarse_diagonal.shape, f32),
+            pltpu.SemaphoreType.DMA((6,)),
             pltpu.VMEM((blocks, side, side), f32),
+            pltpu.VMEM((blocks, side, 2 * side), jnp.bfloat16),
             pltpu.VMEM((blocks,) + tile, f32),
             pltpu.VMEM((groups,) + tile, i32),
             pltpu.VMEM((groups,) + tile, i32),
@@ -513,6 +542,7 @@
             collective_id=0, has_side_effects=True, vmem_limit_bytes=32 << 20
         ),
     )(
+        *(pltpu.with_memory_space_constraint(a, pltpu.HBM) for a in (
         right_side,
         coefficient_index,
         material_coefficients.reshape(1, -1),
@@ -520,7 +550,16 @@
         block_inverses.reshape(blocks, side, side),
         aggregate_map,
         coarse_diagonal,
+        ))
     )
+    return pl.pallas_call(
+        emit,
+        out_shape=(field, field, field),
+        in_specs=[vmem] * 3,
+        out_specs=(hbm,) * 3,
+        scratch_shapes=[pltpu.SemaphoreType.DMA((3,))],
+        compiler_params=pltpu.CompilerParams(vmem_limit_bytes=1 << 20),
+    )(*results)
 
 
 def solution(mesh):

time: 46.2 us -> 34 us (0.74)
  local copies, waits for them, and re-layouts: 8.37 us -> 0 us
  Pallas kernels: 36.7 us -> 33.2 us
    unnamed x17 -> x0, local copies, waits for them, and re-layouts: 8.37 us -> none
    pallas_call x1, Pallas kernels: 36.7 us -> 32.6 us  [shards(): pl.pallas_call(functools.partial(kernel, owners, members), out_shape=(fie...]
    pallas_call x0 -> x1, Pallas kernels: none -> 0.67 us  [shards(): pl.pallas_call(emit, out_shape=(field, field, field), in_specs=[vmem] * 3...]
where the time goes in v2:
time: 34 us; the launch traced here: 33.9 us
  Pallas kernels  33.2 us (98%)
  between operations  0.64 us (2%)
    pallas_call x1, Pallas kernels, shards(): pl.pallas_call(functools.partial(kernel, owners, members), out_shape=(fie...  32.6 us

profile of v2, /device:TPU:0, one launch (start us, length us, event | category | flops | bytes accessed | tf_op | source)
XLA Modules:
  0.0 33.9 jit_solution(3520438001047097953)
XLA Ops:
  0.6 32.6 %shard_map.94 = (f32[8,8,128]{2,1,0:T(8,128)S(1)}, f32[8,8,128]{2,1,0:T(8,128)S(1)}, f32[8,8,128]{2,1,0:T(8,128)S(1)}) custom-call(f32[8,8,128]{2,1,0:T(8,128)} %r_hbm.1, s32[8,8,128]{2,1,0:T(8,128)} %cidx_hbm.1, f32[1,16]{1,0:T(1,128)} %bitcast.5, s32[8,8,128]{2,1,0:T(8,128)} %bitcast.4, f32[64,128,128]{2,1,0:T(8,128)} %bitcast.3, s32[8,8,128]{2,1,0:T(8,128)} %amap_hbm.1, ...), custom_call_target="tpu_custom_call" | custom-call | tf_op jit(solution)/shard_map/pallas_call | solution.py:496
  33.2 0.7 %shard_map.95 = (f32[8,8,128]{2,1,0:T(8,128)}, f32[8,8,128]{2,1,0:T(8,128)}, f32[8,8,128]{2,1,0:T(8,128)}) custom-call(f32[8,8,128]{2,1,0:T(8,128)S(1)} %get-tuple-element.6.x_ref, f32[8,8,128]{2,1,0:T(8,128)S(1)} %get-tuple-element.7.r_ref, f32[8,8,128]{2,1,0:T(8,128)S(1)} %get-tuple-element.8.p_ref), custom_call_target="tpu_custom_call" | custom-call | tf_op jit(solution)/shard_map/pallas_call | solution.py:555

commit v3 on v2

--- a/solution.py
+++ b/solution.py
@@ -170,14 +170,16 @@
     def block_apply(values, done_with_dot, first=False):
         load_turns(values)
 
-        def one(u, dot):
+        def one(u, carry):
+            dot, picked = carry
             if first:
                 mat_copy(u).wait()
                 for b in range(SUB):
                     high, low = split(mats[u * SUB + b])
                     halves[u * SUB + b, :, 0:LANES] = high
                     halves[u * SUB + b, :, LANES : 2 * LANES] = low
-            picked = permuted(key_in[u], lane_in[u])
+            ahead = lax.rem(u + 1, groups)
+            upcoming = permuted(key_in[ahead], lane_in[ahead])
             left = jnp.concatenate(split(picked), axis=0)
             product = zero
             for b in range(SUB):
@@ -186,17 +188,18 @@
                 line = line + both[SUB:, LANES:]
                 product = jnp.where(sub == b, line, product)
             moved[u] = product
-            return dot + picked * product
-
-        dot = lax.fori_loop(0, groups, one, zero)
+            return dot + picked * product, upcoming
+
+        dot, _ = lax.fori_loop(0, groups, one, (zero, permuted(key_in[0], lane_in[0])))
         done_with_dot(total_of(dot))
         load_turns([moved[g] for g in range(groups)])
 
         def back(g, carry):
-            moved[g] = permuted(key_out[g], lane_out[g])
+            for at in (2 * g, 2 * g + 1):
+                moved[at] = permuted(key_out[at], lane_out[at])
             return carry
 
-        lax.fori_loop(0, groups, back, 0)
+        lax.fori_loop(0, groups // 2, back, 0)
         return [moved[g] for g in range(groups)]
 
     base = lax.shift_right_logical(lane, 3)

time: 34 us -> 31.4 us (0.924)
  Pallas kernels: 33.2 us -> 30.6 us
    pallas_call x1, Pallas kernels: 32.6 us -> 30 us  [shards(): pl.pallas_call(functools.partial(kernel, owners, members), out_shape=(fie...]
where the time goes in v3:
time: 31.4 us; the launch traced here: 31.3 us
  Pallas kernels  30.6 us (97%)
  between operations  0.64 us (2%)
    pallas_call x1, Pallas kernels, shards(): pl.pallas_call(functools.partial(kernel, owners, members), out_shape=(fie...  30 us
    pallas_call x1, Pallas kernels, shards(): pl.pallas_call(emit, out_shape=(field, field, field), in_specs=[vmem] * 3...  0.67 us

profile of v3, /device:TPU:0, one launch (start us, length us, event | category | flops | bytes accessed | tf_op | source)
XLA Modules:
  0.0 31.3 jit_solution(18045604856792324452)
XLA Ops:
  0.6 30.0 %shard_map.94 = (f32[8,8,128]{2,1,0:T(8,128)S(1)}, f32[8,8,128]{2,1,0:T(8,128)S(1)}, f32[8,8,128]{2,1,0:T(8,128)S(1)}) custom-call(f32[8,8,128]{2,1,0:T(8,128)} %r_hbm.1, s32[8,8,128]{2,1,0:T(8,128)} %cidx_hbm.1, f32[1,16]{1,0:T(1,128)} %bitcast.5, s32[8,8,128]{2,1,0:T(8,128)} %bitcast.4, f32[64,128,128]{2,1,0:T(8,128)} %bitcast.3, s32[8,8,128]{2,1,0:T(8,128)} %amap_hbm.1, ...), custom_call_target="tpu_custom_call" | custom-call | tf_op jit(solution)/shard_map/pallas_call | solution.py:499
  30.6 0.7 %shard_map.95 = (f32[8,8,128]{2,1,0:T(8,128)}, f32[8,8,128]{2,1,0:T(8,128)}, f32[8,8,128]{2,1,0:T(8,128)}) custom-call(f32[8,8,128]{2,1,0:T(8,128)S(1)} %get-tuple-element.6.x_ref, f32[8,8,128]{2,1,0:T(8,128)S(1)} %get-tuple-element.7.r_ref, f32[8,8,128]{2,1,0:T(8,128)S(1)} %get-tuple-element.8.p_ref), custom_call_target="tpu_custom_call" | custom-call | tf_op jit(solution)/shard_map/pallas_call | solution.py:558

commit v4 on v3

--- a/solution.py
+++ b/solution.py
@@ -17,6 +17,7 @@
 MAIN = 8
 XLO, XHI, ZLO, ZHI, CORNER = 8, 9, 10, 11, 12
 SLOTS = 13
+AHEAD = 4
 DIRECTIONS = ((-1, 0), (1, 0), (0, -1), (0, 1), (-1, -1), (-1, 1), (1, -1), (1, 1))
 
 
@@ -170,36 +171,44 @@
     def block_apply(values, done_with_dot, first=False):
         load_turns(values)
 
-        def one(u, carry):
+        def some(turn, carry):
             dot, picked = carry
             if first:
-                mat_copy(u).wait()
+                for at in range(AHEAD):
+                    mat_copy(turn * AHEAD + at).wait()
+            for at in range(AHEAD):
+                u = turn * AHEAD + at
+                if first:
+                    for b in range(SUB):
+                        high, low = split(mats[u * SUB + b])
+                        halves[u * SUB + b, :, 0:LANES] = high
+                        halves[u * SUB + b, :, LANES : 2 * LANES] = low
+                ahead = lax.rem(u + 1, groups)
+                upcoming = permuted(key_in[ahead], lane_in[ahead])
+                left = jnp.concatenate(split(picked), axis=0)
+                product = zero
                 for b in range(SUB):
-                    high, low = split(mats[u * SUB + b])
-                    halves[u * SUB + b, :, 0:LANES] = high
-                    halves[u * SUB + b, :, LANES : 2 * LANES] = low
-            ahead = lax.rem(u + 1, groups)
-            upcoming = permuted(key_in[ahead], lane_in[ahead])
-            left = jnp.concatenate(split(picked), axis=0)
-            product = zero
-            for b in range(SUB):
-                both = jnp.dot(left, halves[u * SUB + b], preferred_element_type=jnp.float32)
-                line = both[:SUB, :LANES] + (both[SUB:, :LANES] + both[:SUB, LANES:])
-                line = line + both[SUB:, LANES:]
-                product = jnp.where(sub == b, line, product)
-            moved[u] = product
-            return dot + picked * product, upcoming
-
-        dot, _ = lax.fori_loop(0, groups, one, (zero, permuted(key_in[0], lane_in[0])))
+                    both = jnp.dot(left, halves[u * SUB + b], preferred_element_type=jnp.float32)
+                    line = both[:SUB, :LANES] + (both[SUB:, :LANES] + both[:SUB, LANES:])
+                    line = line + both[SUB:, LANES:]
+                    product = jnp.where(sub == b, line, product)
+                moved[u] = product
+                dot = dot + picked * product
+                picked = upcoming
+            return dot, picked
+
+        dot, _ = lax.fori_loop(
+            0, groups // AHEAD, some, (zero, permuted(key_in[0], lane_in[0]))
+        )
         done_with_dot(total_of(dot))
         load_turns([moved[g] for g in range(groups)])
 
         def back(g, carry):
-            for at in (2 * g, 2 * g + 1):
+            for at in (4 * g, 4 * g + 1, 4 * g + 2, 4 * g + 3):
                 moved[at] = permuted(key_out[at], lane_out[at])
             return carry
 
-        lax.fori_loop(0, groups // 2, back, 0)
+        lax.fori_loop(0, groups // 4, back, 0)
         return [moved[g] for g in range(groups)]
 
     base = lax.shift_right_logical(lane, 3)

time: 31.4 us -> 29.5 us (0.939)
  Pallas kernels: 30.6 us -> 28.7 us
    pallas_call x1, Pallas kernels: 30 us -> 28 us  [shards(): pl.pallas_call(functools.partial(kernel, owners, members), out_shape=(fie...]
where the time goes in v4:
time: 29.5 us; the launch traced here: 29.3 us
  Pallas kernels  28.7 us (97%)
  between operations  0.64 us (2%)
    pallas_call x1, Pallas kernels, shards(): pl.pallas_call(functools.partial(kernel, owners, members), out_shape=(fie...  28 us
    pallas_call x1, Pallas kernels, shards(): pl.pallas_call(emit, out_shape=(field, field, field), in_specs=[vmem] * 3...  0.67 us

profile of v4, /device:TPU:0, one launch (start us, length us, event | category | flops | bytes accessed | tf_op | source)
XLA Modules:
  0.0 29.3 jit_solution(6795088978292169577)
XLA Ops:
  0.6 28.0 %shard_map.94 = (f32[8,8,128]{2,1,0:T(8,128)S(1)}, f32[8,8,128]{2,1,0:T(8,128)S(1)}, f32[8,8,128]{2,1,0:T(8,128)S(1)}) custom-call(f32[8,8,128]{2,1,0:T(8,128)} %r_hbm.1, s32[8,8,128]{2,1,0:T(8,128)} %cidx_hbm.1, f32[1,16]{1,0:T(1,128)} %bitcast.5, s32[8,8,128]{2,1,0:T(8,128)} %bitcast.4, f32[64,128,128]{2,1,0:T(8,128)} %bitcast.3, s32[8,8,128]{2,1,0:T(8,128)} %amap_hbm.1, ...), custom_call_target="tpu_custom_call" | custom-call | tf_op jit(solution)/shard_map/pallas_call | solution.py:508
  28.7 0.7 %shard_map.95 = (f32[8,8,128]{2,1,0:T(8,128)}, f32[8,8,128]{2,1,0:T(8,128)}, f32[8,8,128]{2,1,0:T(8,128)}) custom-call(f32[8,8,128]{2,1,0:T(8,128)S(1)} %get-tuple-element.6.x_ref, f32[8,8,128]{2,1,0:T(8,128)S(1)} %get-tuple-element.7.r_ref, f32[8,8,128]{2,1,0:T(8,128)S(1)} %get-tuple-element.8.p_ref), custom_call_target="tpu_custom_call" | custom-call | tf_op jit(solution)/shard_map/pallas_call | solution.py:567

commit v5 on v4

--- a/solution.py
+++ b/solution.py
@@ -17,7 +17,7 @@
 MAIN = 8
 XLO, XHI, ZLO, ZHI, CORNER = 8, 9, 10, 11, 12
 SLOTS = 13
-AHEAD = 4
+AHEAD = 8
 DIRECTIONS = ((-1, 0), (1, 0), (0, -1), (0, 1), (-1, -1), (-1, 1), (1, -1), (1, 1))
 
 
@@ -124,7 +124,7 @@
     taller = lax.broadcasted_iota(jnp.int32, (LANES, LANES), 0)
     wide = lax.broadcasted_iota(jnp.int32, (groups * SUB, LANES), 1).astype(jnp.float32)
 
-    def find(g, carry):
+    def find_one(g, carry):
         block = cells_ref[g]
         for b in range(SUB):
             source = block[b : b + 1, :]
@@ -141,8 +141,11 @@
             )
         return carry
 
+    def find(turn, carry):
+        return find_one(2 * turn + 1, find_one(2 * turn, carry))
+
     found = lax.fori_loop(
-        0, groups, find, jnp.zeros((2 * groups * SUB, LANES), jnp.float32)
+        0, groups // 2, find, jnp.zeros((2 * groups * SUB, LANES), jnp.float32)
     ).astype(jnp.int32)
     for g in range(groups):
         block = found[g * SUB : (g + 1) * SUB]
@@ -204,11 +207,12 @@
         load_turns([moved[g] for g in range(groups)])
 
         def back(g, carry):
-            for at in (4 * g, 4 * g + 1, 4 * g + 2, 4 * g + 3):
+            for step in range(AHEAD):
+                at = g * AHEAD + step
                 moved[at] = permuted(key_out[at], lane_out[at])
             return carry
 
-        lax.fori_loop(0, groups // 4, back, 0)
+        lax.fori_loop(0, groups // AHEAD, back, 0)
         return [moved[g] for g in range(groups)]
 
     base = lax.shift_right_logical(lane, 3)

time: 29.5 us -> 28.1 us (0.953)
  Pallas kernels: 28.7 us -> 27.3 us
    pallas_call x1, Pallas kernels: 28 us -> 26.7 us  [shards(): pl.pallas_call(functools.partial(kernel, owners, members), out_shape=(fie...]
where the time goes in v5:
time: 28.1 us; the launch traced here: 28 us
  Pallas kernels  27.3 us (97%)
  between operations  0.64 us (2%)
    pallas_call x1, Pallas kernels, shards(): pl.pallas_call(functools.partial(kernel, owners, members), out_shape=(fie...  26.7 us
    pallas_call x1, Pallas kernels, shards(): pl.pallas_call(emit, out_shape=(field, field, field), in_specs=[vmem] * 3...  0.67 us

profile of v5, /device:TPU:0, one launch (start us, length us, event | category | flops | bytes accessed | tf_op | source)
XLA Modules:
  0.0 28.0 jit_solution(16179340176108874154)
XLA Ops:
  0.6 26.7 %shard_map.94 = (f32[8,8,128]{2,1,0:T(8,128)S(1)}, f32[8,8,128]{2,1,0:T(8,128)S(1)}, f32[8,8,128]{2,1,0:T(8,128)S(1)}) custom-call(f32[8,8,128]{2,1,0:T(8,128)} %r_hbm.1, s32[8,8,128]{2,1,0:T(8,128)} %cidx_hbm.1, f32[1,16]{1,0:T(1,128)} %bitcast.5, s32[8,8,128]{2,1,0:T(8,128)} %bitcast.4, f32[64,128,128]{2,1,0:T(8,128)} %bitcast.3, s32[8,8,128]{2,1,0:T(8,128)} %amap_hbm.1, ...), custom_call_target="tpu_custom_call" | custom-call | tf_op jit(solution)/shard_map/pallas_call | solution.py:512
  27.3 0.7 %shard_map.95 = (f32[8,8,128]{2,1,0:T(8,128)}, f32[8,8,128]{2,1,0:T(8,128)}, f32[8,8,128]{2,1,0:T(8,128)}) custom-call(f32[8,8,128]{2,1,0:T(8,128)S(1)} %get-tuple-element.6.x_ref, f32[8,8,128]{2,1,0:T(8,128)S(1)} %get-tuple-element.7.r_ref, f32[8,8,128]{2,1,0:T(8,128)S(1)} %get-tuple-element.8.p_ref), custom_call_target="tpu_custom_call" | custom-call | tf_op jit(solution)/shard_map/pallas_call | solution.py:571
